TPU v7x, 512 devices: a whole 4x8x8 slice. The times are simulated.
512 devices in a mesh: tm: 32 (over y, x), blk: 16 (over z, core).
Axes of the slice: x: 4, y: 8, z: 8, core: 2. Of those that a mesh axis runs over, the one named last changes fastest.
Arguments:
- panel_strip: bfloat16 [32, 8192, 2304], P('tm', 'blk'), may hold values from -6 to 6
- pivot_inverses: bfloat16 [32, 2, 256, 256], P('tm'), may hold values from -0.0234375 to 0.0234375
- coupling: float32 [32, 256, 256], P('tm'), may hold values from -0.375 to 0.375
- pivot_nodes: int32 [3, 256], replicated, may hold values from 0 to 8191, as said below
Outputs:
- trailing: bfloat16 [32, 8192, 1792], P('tm', 'blk')
- reduced: float32 [32, 256, 256], P('tm')
Inputs may be any that keep to these rules, and one draw needn't show every extreme that they name: `pivot_nodes`: entry j of every row is a node of the range [(j // 16) * 512, (j // 16 + 1) * 512); all 768 entries differ.
All inputs are finite; a program needn't handle non-finite values.
Results may differ from a plain program's by a relative error of at most 0.0068.
Values may be sent and summed in bfloat16 or wider, within the bound.
No kernel may reach another device: no remote copies, remote signals or barrier semaphores. Data moves between devices by JAX's collectives and lax.ppermute only.
A program may use at most 128 MiB of HBM per device.

v0:
```python
import jax
import jax.numpy as jnp
from jax import lax
from jax.sharding import PartitionSpec as P


def passed_along(x, axis, by):
    count = lax.axis_size(axis)
    pairs = [(i, i + by) for i in range(count) if 0 <= i + by < count]
    return lax.ppermute(x, axis, pairs)


def matmul_high(left, right):
    return jnp.dot(left, right, precision=lax.Precision.HIGHEST, preferred_element_type=jnp.float32)


def body(panel_strip, pivot_inverses, coupling, pivot_nodes):
    strip_block = panel_strip[0]
    inverse_pair = pivot_inverses[0]
    coupling_here = coupling[0]
    panel_width = inverse_pair.shape[-1]
    rows_here = strip_block.shape[0]
    blk_count = lax.axis_size("blk")
    per_device = panel_width // blk_count
    my_index = lax.axis_index("blk")
    local_rows = (
        lax.dynamic_slice_in_dim(pivot_nodes, my_index * per_device, per_device, 1)
        - my_index * rows_here
    )
    picker = (
        local_rows[:, :, None] == lax.broadcasted_iota(jnp.int32, (3, per_device, rows_here), 2)
    ).astype(jnp.bfloat16)
    factor_one = jnp.dot(
        strip_block[:, :panel_width], inverse_pair[0], preferred_element_type=jnp.float32
    ).astype(jnp.bfloat16)
    picked_one = jnp.dot(
        picker[0], strip_block[:, panel_width:], preferred_element_type=jnp.float32
    ).astype(jnp.bfloat16)
    columns = factor_one
    updated = (
        strip_block[:, panel_width:].astype(jnp.float32)
        - jnp.dot(
            columns,
            lax.all_gather(picked_one, "blk", axis=0, tiled=True),
            preferred_element_type=jnp.float32,
        )
    ).astype(jnp.bfloat16)
    factor_two = jnp.dot(
        updated[:, :panel_width], inverse_pair[1], preferred_element_type=jnp.float32
    ).astype(jnp.bfloat16)
    picked_two = jnp.dot(
        picker[1], updated[:, panel_width:], preferred_element_type=jnp.float32
    ).astype(jnp.bfloat16)
    columns = factor_two
    trailing = (
        updated[:, panel_width:].astype(jnp.float32)
        - jnp.dot(
            columns,
            lax.all_gather(picked_two, "blk", axis=0, tiled=True),
            preferred_element_type=jnp.float32,
        )
    ).astype(jnp.bfloat16)
    edge_rows = jnp.dot(
        picker[2], trailing[:, :panel_width], preferred_element_type=jnp.float32
    ).astype(jnp.bfloat16)
    boundary_block = lax.all_gather(edge_rows, "blk", axis=0, tiled=True).astype(jnp.float32)
    position = lax.axis_index("tm")

    def advance(turn_index, current):
        incoming = passed_along(current, "tm", 1)

        def apply_map(operand):
            return (
                matmul_high(matmul_high(coupling_here, operand), coupling_here.T) + boundary_block
            )

        def keep_state(operand):
            return current

        return lax.cond(position == turn_index, apply_map, keep_state, incoming)

    reduced = lax.fori_loop(1, lax.axis_size("tm"), advance, boundary_block)
    return (trailing[None], reduced[None])


def solution(mesh):
    placed = (P("tm", "blk", None), P("tm", None, None, None), P("tm", None, None), P())
    return jax.shard_map(
        body,
        mesh=mesh,
        in_specs=placed,
        out_specs=(P("tm", "blk", None), P("tm", None, None)),
        check_vma=False,
    )
```

profile of v0, /device:TPU:32, one launch (start us, length us, event | category | flops | bytes accessed | tf_op | source)
XLA Modules:
  0.0 484.5 jit_solution(10073837723274590851)
XLA Ops:
  8.1 2.6 convolution_convert_fusion.1
  10.7 46.4 %all-gather.2.cloned.1.call-done = bf16[256,2048]{1,0:T(8,128)(2,1)} async-done(((bf16[16,2048]{1,0:T(8,128)(2,1)}), bf16[256,2048]{1,0:T(8,128)(2,1)}) %all-gather.2.cloned.1.call-update) | async-done | bytes 1048592 | tf_op jit(solution)/shard_map/all_gather | solution.py:44
  57.1 2.8 subtract_convert_fusion
  60.3 18.0 %all_gather.10 = bf16[256,1792]{1,0:T(8,128)(2,1)S(1)} all-gather(bf16[16,1792]{1,0:T(8,128)(2,1)S(1)} %convolution_convert_fusion), channel_id=1, replica_groups=mesh['tm'=32,'blk'=16] {'blk'}, dimensions={0}, use_global_device_ids=true | all-gather | bytes 974848 | tf_op jit(solution)/shard_map/all_gather | solution.py:59
  78.3 3.0 subtract_convert_fusion.1
  82.4 15.1 %all_gather.11 = bf16[256,256]{1,0:T(8,128)(2,1)S(1)} all-gather(bf16[16,256]{1,0:T(8,128)(2,1)S(1)} %convolution_convert_fusion.4), channel_id=1, replica_groups=mesh['tm'=32,'blk'=16] {'blk'}, dimensions={0}, use_global_device_ids=true | all-gather | bytes 139264 | tf_op jit(solution)/shard_map/all_gather | solution.py:66
  97.6 379.3 %while.16 = (s32[]{:T(128)}, f32[256,256]{1,0:T(8,128)S(1)}, s32[]{:T(128)}, f32[256,256]{1,0:T(8,128)S(1)}, f32[256,256]{1,0:T(8,128)S(1)}, /*index=5*/s32[]{:T(128)}) while((s32[]{:T(128)}, f32[256,256]{1,0:T(8,128)S(1)}, s32[]{:T(128)}, f32[256,256]{1,0:T(8,128)S(1)}, f32[256,256]{1,0:T(8,128)S(1)}, /*index=5*/s32[]{:T(128)}) %tuple.51), condition=%wide.region_3.0_spmd, body=%wide.region_0.0_spmd.sunk | while | flops 402718720 | bytes 2883739 | solution.py:82
  97.6 3.4 collective-permute-start
  101.0 10.4 %collective-permute-done = f32[256,256]{1,0:T(8,128)S(1)} collective-permute-done((f32[256,256]{1,0:T(8,128)S(1)}, f32[256,256]{1,0:T(8,128)S(1)}, u32[]{:S(2)}, u32[]{:S(2)}) %collective-permute-start) | collective-permute-done | bytes 262176 | tf_op jit(solution)/shard_map/while/body/eval_jaxpr/ppermute | solution.py:10
  111.4 1.9 collective-permute-start
  113.3 11.0 %collective-permute-done = f32[256,256]{1,0:T(8,128)S(1)} collective-permute-done((f32[256,256]{1,0:T(8,128)S(1)}, f32[256,256]{1,0:T(8,128)S(1)}, u32[]{:S(2)}, u32[]{:S(2)}) %collective-permute-start) | collective-permute-done | bytes 262176 | tf_op jit(solution)/shard_map/while/body/eval_jaxpr/ppermute | solution.py:10
  124.3 1.9 collective-permute-start
  126.3 10.1 %collective-permute-done = f32[256,256]{1,0:T(8,128)S(1)} collective-permute-done((f32[256,256]{1,0:T(8,128)S(1)}, f32[256,256]{1,0:T(8,128)S(1)}, u32[]{:S(2)}, u32[]{:S(2)}) %collective-permute-start) | collective-permute-done | bytes 262176 | tf_op jit(solution)/shard_map/while/body/eval_jaxpr/ppermute | solution.py:10
  136.4 1.9 collective-permute-start
  138.3 9.7 %collective-permute-done = f32[256,256]{1,0:T(8,128)S(1)} collective-permute-done((f32[256,256]{1,0:T(8,128)S(1)}, f32[256,256]{1,0:T(8,128)S(1)}, u32[]{:S(2)}, u32[]{:S(2)}) %collective-permute-start) | collective-permute-done | bytes 262176 | tf_op jit(solution)/shard_map/while/body/eval_jaxpr/ppermute | solution.py:10
  147.9 1.9 collective-permute-start
  149.9 9.7 %collective-permute-done = f32[256,256]{1,0:T(8,128)S(1)} collective-permute-done((f32[256,256]{1,0:T(8,128)S(1)}, f32[256,256]{1,0:T(8,128)S(1)}, u32[]{:S(2)}, u32[]{:S(2)}) %collective-permute-start) | collective-permute-done | bytes 262176 | tf_op jit(solution)/shard_map/while/body/eval_jaxpr/ppermute | solution.py:10
  159.5 1.9 collective-permute-start
  161.4 9.7 %collective-permute-done = f32[256,256]{1,0:T(8,128)S(1)} collective-permute-done((f32[256,256]{1,0:T(8,128)S(1)}, f32[256,256]{1,0:T(8,128)S(1)}, u32[]{:S(2)}, u32[]{:S(2)}) %collective-permute-start) | collective-permute-done | bytes 262176 | tf_op jit(solution)/shard_map/while/body/eval_jaxpr/ppermute | solution.py:10
  171.1 1.9 collective-permute-start
  173.0 9.7 %collective-permute-done = f32[256,256]{1,0:T(8,128)S(1)} collective-permute-done((f32[256,256]{1,0:T(8,128)S(1)}, f32[256,256]{1,0:T(8,128)S(1)}, u32[]{:S(2)}, u32[]{:S(2)}) %collective-permute-start) | collective-permute-done | bytes 262176 | tf_op jit(solution)/shard_map/while/body/eval_jaxpr/ppermute | solution.py:10
  182.7 1.9 collective-permute-start
  184.6 9.8 %collective-permute-done = f32[256,256]{1,0:T(8,128)S(1)} collective-permute-done((f32[256,256]{1,0:T(8,128)S(1)}, f32[256,256]{1,0:T(8,128)S(1)}, u32[]{:S(2)}, u32[]{:S(2)}) %collective-permute-start) | collective-permute-done | bytes 262176 | tf_op jit(solution)/shard_map/while/body/eval_jaxpr/ppermute | solution.py:10
  194.4 1.9 collective-permute-start
  196.3 10.9 %collective-permute-done = f32[256,256]{1,0:T(8,128)S(1)} collective-permute-done((f32[256,256]{1,0:T(8,128)S(1)}, f32[256,256]{1,0:T(8,128)S(1)}, u32[]{:S(2)}, u32[]{:S(2)}) %collective-permute-start) | collective-permute-done | bytes 262176 | tf_op jit(solution)/shard_map/while/body/eval_jaxpr/ppermute | solution.py:10
  207.3 1.9 collective-permute-start
  209.2 12.1 %collective-permute-done = f32[256,256]{1,0:T(8,128)S(1)} collective-permute-done((f32[256,256]{1,0:T(8,128)S(1)}, f32[256,256]{1,0:T(8,128)S(1)}, u32[]{:S(2)}, u32[]{:S(2)}) %collective-permute-start) | collective-permute-done | bytes 262176 | tf_op jit(solution)/shard_map/while/body/eval_jaxpr/ppermute | solution.py:10
  221.3 1.9 collective-permute-start
  223.3 11.6 %collective-permute-done = f32[256,256]{1,0:T(8,128)S(1)} collective-permute-done((f32[256,256]{1,0:T(8,128)S(1)}, f32[256,256]{1,0:T(8,128)S(1)}, u32[]{:S(2)}, u32[]{:S(2)}) %collective-permute-start) | collective-permute-done | bytes 262176 | tf_op jit(solution)/shard_map/while/body/eval_jaxpr/ppermute | solution.py:10
  234.9 1.9 collective-permute-start
  236.8 10.8 %collective-permute-done = f32[256,256]{1,0:T(8,128)S(1)} collective-permute-done((f32[256,256]{1,0:T(8,128)S(1)}, f32[256,256]{1,0:T(8,128)S(1)}, u32[]{:S(2)}, u32[]{:S(2)}) %collective-permute-start) | collective-permute-done | bytes 262176 | tf_op jit(solution)/shard_map/while/body/eval_jaxpr/ppermute | solution.py:10
  247.6 1.9 collective-permute-start
  249.5 9.9 %collective-permute-done = f32[256,256]{1,0:T(8,128)S(1)} collective-permute-done((f32[256,256]{1,0:T(8,128)S(1)}, f32[256,256]{1,0:T(8,128)S(1)}, u32[]{:S(2)}, u32[]{:S(2)}) %collective-permute-start) | collective-permute-done | bytes 262176 | tf_op jit(solution)/shard_map/while/body/eval_jaxpr/ppermute | solution.py:10
  259.4 1.9 collective-permute-start
  261.3 9.7 %collective-permute-done = f32[256,256]{1,0:T(8,128)S(1)} collective-permute-done((f32[256,256]{1,0:T(8,128)S(1)}, f32[256,256]{1,0:T(8,128)S(1)}, u32[]{:S(2)}, u32[]{:S(2)}) %collective-permute-start) | collective-permute-done | bytes 262176 | tf_op jit(solution)/shard_map/while/body/eval_jaxpr/ppermute | solution.py:10
  271.0 1.9 collective-permute-start
  272.9 9.7 %collective-permute-done = f32[256,256]{1,0:T(8,128)S(1)} collective-permute-done((f32[256,256]{1,0:T(8,128)S(1)}, f32[256,256]{1,0:T(8,128)S(1)}, u32[]{:S(2)}, u32[]{:S(2)}) %collective-permute-start) | collective-permute-done | bytes 262176 | tf_op jit(solution)/shard_map/while/body/eval_jaxpr/ppermute | solution.py:10
  282.5 1.9 collective-permute-start
  284.5 9.7 %collective-permute-done = f32[256,256]{1,0:T(8,128)S(1)} collective-permute-done((f32[256,256]{1,0:T(8,128)S(1)}, f32[256,256]{1,0:T(8,128)S(1)}, u32[]{:S(2)}, u32[]{:S(2)}) %collective-permute-start) | collective-permute-done | bytes 262176 | tf_op jit(solution)/shard_map/while/body/eval_jaxpr/ppermute | solution.py:10
  294.9 1.9 collective-permute-start
  296.9 9.7 %collective-permute-done = f32[256,256]{1,0:T(8,128)S(1)} collective-permute-done((f32[256,256]{1,0:T(8,128)S(1)}, f32[256,256]{1,0:T(8,128)S(1)}, u32[]{:S(2)}, u32[]{:S(2)}) %collective-permute-start) | collective-permute-done | bytes 262176 | tf_op jit(solution)/shard_map/while/body/eval_jaxpr/ppermute | solution.py:10
  306.5 1.9 collective-permute-start
  308.4 10.1 %collective-permute-done = f32[256,256]{1,0:T(8,128)S(1)} collective-permute-done((f32[256,256]{1,0:T(8,128)S(1)}, f32[256,256]{1,0:T(8,128)S(1)}, u32[]{:S(2)}, u32[]{:S(2)}) %collective-permute-start) | collective-permute-done | bytes 262176 | tf_op jit(solution)/shard_map/while/body/eval_jaxpr/ppermute | solution.py:10
  318.5 1.9 collective-permute-start
  320.4 11.2 %collective-permute-done = f32[256,256]{1,0:T(8,128)S(1)} collective-permute-done((f32[256,256]{1,0:T(8,128)S(1)}, f32[256,256]{1,0:T(8,128)S(1)}, u32[]{:S(2)}, u32[]{:S(2)}) %collective-permute-start) | collective-permute-done | bytes 262176 | tf_op jit(solution)/shard_map/while/body/eval_jaxpr/ppermute | solution.py:10
  331.6 1.9 collective-permute-start
  333.6 12.3 %collective-permute-done = f32[256,256]{1,0:T(8,128)S(1)} collective-permute-done((f32[256,256]{1,0:T(8,128)S(1)}, f32[256,256]{1,0:T(8,128)S(1)}, u32[]{:S(2)}, u32[]{:S(2)}) %collective-permute-start) | collective-permute-done | bytes 262176 | tf_op jit(solution)/shard_map/while/body/eval_jaxpr/ppermute | solution.py:10
  345.9 1.9 collective-permute-start
  347.8 11.6 %collective-permute-done = f32[256,256]{1,0:T(8,128)S(1)} collective-permute-done((f32[256,256]{1,0:T(8,128)S(1)}, f32[256,256]{1,0:T(8,128)S(1)}, u32[]{:S(2)}, u32[]{:S(2)}) %collective-permute-start) | collective-permute-done | bytes 262176 | tf_op jit(solution)/shard_map/while/body/eval_jaxpr/ppermute | solution.py:10
  359.4 1.9 collective-permute-start
  361.3 10.8 %collective-permute-done = f32[256,256]{1,0:T(8,128)S(1)} collective-permute-done((f32[256,256]{1,0:T(8,128)S(1)}, f32[256,256]{1,0:T(8,128)S(1)}, u32[]{:S(2)}, u32[]{:S(2)}) %collective-permute-start) | collective-permute-done | bytes 262176 | tf_op jit(solution)/shard_map/while/body/eval_jaxpr/ppermute | solution.py:10
  372.1 1.9 collective-permute-start
  374.0 9.8 %collective-permute-done = f32[256,256]{1,0:T(8,128)S(1)} collective-permute-done((f32[256,256]{1,0:T(8,128)S(1)}, f32[256,256]{1,0:T(8,128)S(1)}, u32[]{:S(2)}, u32[]{:S(2)}) %collective-permute-start) | collective-permute-done | bytes 262176 | tf_op jit(solution)/shard_map/while/body/eval_jaxpr/ppermute | solution.py:10
  383.9 1.9 collective-permute-start
  385.8 9.7 %collective-permute-done = f32[256,256]{1,0:T(8,128)S(1)} collective-permute-done((f32[256,256]{1,0:T(8,128)S(1)}, f32[256,256]{1,0:T(8,128)S(1)}, u32[]{:S(2)}, u32[]{:S(2)}) %collective-permute-start) | collective-permute-done | bytes 262176 | tf_op jit(solution)/shard_map/while/body/eval_jaxpr/ppermute | solution.py:10
  395.5 1.9 collective-permute-start
  397.4 9.7 %collective-permute-done = f32[256,256]{1,0:T(8,128)S(1)} collective-permute-done((f32[256,256]{1,0:T(8,128)S(1)}, f32[256,256]{1,0:T(8,128)S(1)}, u32[]{:S(2)}, u32[]{:S(2)}) %collective-permute-start) | collective-permute-done | bytes 262176 | tf_op jit(solution)/shard_map/while/body/eval_jaxpr/ppermute | solution.py:10
  407.0 1.9 collective-permute-start
  409.0 9.7 %collective-permute-done = f32[256,256]{1,0:T(8,128)S(1)} collective-permute-done((f32[256,256]{1,0:T(8,128)S(1)}, f32[256,256]{1,0:T(8,128)S(1)}, u32[]{:S(2)}, u32[]{:S(2)}) %collective-permute-start) | collective-permute-done | bytes 262176 | tf_op jit(solution)/shard_map/while/body/eval_jaxpr/ppermute | solution.py:10
  420.5 9.7 %collective-permute-done = f32[256,256]{1,0:T(8,128)S(1)} collective-permute-done((f32[256,256]{1,0:T(8,128)S(1)}, f32[256,256]{1,0:T(8,128)S(1)}, u32[]{:S(2)}, u32[]{:S(2)}) %collective-permute-start) | collective-permute-done | bytes 262176 | tf_op jit(solution)/shard_map/while/body/eval_jaxpr/ppermute | solution.py:10
  432.1 10.1 %collective-permute-done = f32[256,256]{1,0:T(8,128)S(1)} collective-permute-done((f32[256,256]{1,0:T(8,128)S(1)}, f32[256,256]{1,0:T(8,128)S(1)}, u32[]{:S(2)}, u32[]{:S(2)}) %collective-permute-start) | collective-permute-done | bytes 262176 | tf_op jit(solution)/shard_map/while/body/eval_jaxpr/ppermute | solution.py:10
  444.1 9.7 %collective-permute-done = f32[256,256]{1,0:T(8,128)S(1)} collective-permute-done((f32[256,256]{1,0:T(8,128)S(1)}, f32[256,256]{1,0:T(8,128)S(1)}, u32[]{:S(2)}, u32[]{:S(2)}) %collective-permute-start) | collective-permute-done | bytes 262176 | tf_op jit(solution)/shard_map/while/body/eval_jaxpr/ppermute | solution.py:10
  455.7 9.7 %collective-permute-done = f32[256,256]{1,0:T(8,128)S(1)} collective-permute-done((f32[256,256]{1,0:T(8,128)S(1)}, f32[256,256]{1,0:T(8,128)S(1)}, u32[]{:S(2)}, u32[]{:S(2)}) %collective-permute-start) | collective-permute-done | bytes 262176 | tf_op jit(solution)/shard_map/while/body/eval_jaxpr/ppermute | solution.py:10
  467.3 9.7 %collective-permute-done = f32[256,256]{1,0:T(8,128)S(1)} collective-permute-done((f32[256,256]{1,0:T(8,128)S(1)}, f32[256,256]{1,0:T(8,128)S(1)}, u32[]{:S(2)}, u32[]{:S(2)}) %collective-permute-start) | collective-permute-done | bytes 262176 | tf_op jit(solution)/shard_map/while/body/eval_jaxpr/ppermute | solution.py:10
  (52 shorter events, 14.3 us)
Async XLA Ops:
  7.2 50.0 %copy-start.2 = (bf16[1,2,256,256]{3,2,1,0:T(8,128)(2,1)S(1)}, bf16[1,2,256,256]{3,2,1,0:T(8,128)(2,1)}, u32[]{:S(2)}) copy-start(bf16[1,2,256,256]{3,2,1,0:T(8,128)(2,1)} %param.9) | copy-start | bytes 786436
  7.2 50.0 %all-gather.2.cloned.1.call-start = ((), (), s32[]{:S(2)}) async-start(), calls=%async_computation | async-start | bytes 1114112 | tf_op jit(solution)/shard_map/all_gather | solution.py:44
  78.3 19.3 %copy-start = (f32[1,256,256]{2,1,0:T(8,128)S(1)}, f32[1,256,256]{2,1,0:T(8,128)}, u32[]{:S(2)}) copy-start(f32[1,256,256]{2,1,0:T(8,128)} %param.10) | copy-start | bytes 786436
  97.6 13.8 %collective-permute-start = (f32[256,256]{1,0:T(8,128)S(1)}, f32[256,256]{1,0:T(8,128)S(1)}, u32[]{:S(2)}, u32[]{:S(2)}) collective-permute-start(f32[256,256]{1,0:T(8,128)S(1)} %get-tuple-element.162), channel_id=1, source_target_pairs={{0,16},{16,32},{32,48},{48,64},{64,80},{80,96},{96,112},{112,128},... | collective-permute-start | bytes 786440 | tf_op jit(solution)/shard_map/while/body/eval_jaxpr/ppermute | solution.py:10
  111.4 13.0 %collective-permute-start = (f32[256,256]{1,0:T(8,128)S(1)}, f32[256,256]{1,0:T(8,128)S(1)}, u32[]{:S(2)}, u32[]{:S(2)}) collective-permute-start(f32[256,256]{1,0:T(8,128)S(1)} %get-tuple-element.162), channel_id=1, source_target_pairs={{0,16},{16,32},{32,48},{48,64},{64,80},{80,96},{96,112},{112,128},... | collective-permute-start | bytes 786440 | tf_op jit(solution)/shard_map/while/body/eval_jaxpr/ppermute | solution.py:10
  124.3 12.0 %collective-permute-start = (f32[256,256]{1,0:T(8,128)S(1)}, f32[256,256]{1,0:T(8,128)S(1)}, u32[]{:S(2)}, u32[]{:S(2)}) collective-permute-start(f32[256,256]{1,0:T(8,128)S(1)} %get-tuple-element.162), channel_id=1, source_target_pairs={{0,16},{16,32},{32,48},{48,64},{64,80},{80,96},{96,112},{112,128},... | collective-permute-start | bytes 786440 | tf_op jit(solution)/shard_map/while/body/eval_jaxpr/ppermute | solution.py:10
  136.4 11.6 %collective-permute-start = (f32[256,256]{1,0:T(8,128)S(1)}, f32[256,256]{1,0:T(8,128)S(1)}, u32[]{:S(2)}, u32[]{:S(2)}) collective-permute-start(f32[256,256]{1,0:T(8,128)S(1)} %get-tuple-element.162), channel_id=1, source_target_pairs={{0,16},{16,32},{32,48},{48,64},{64,80},{80,96},{96,112},{112,128},... | collective-permute-start | bytes 786440 | tf_op jit(solution)/shard_map/while/body/eval_jaxpr/ppermute | solution.py:10
  147.9 11.6 %collective-permute-start = (f32[256,256]{1,0:T(8,128)S(1)}, f32[256,256]{1,0:T(8,128)S(1)}, u32[]{:S(2)}, u32[]{:S(2)}) collective-permute-start(f32[256,256]{1,0:T(8,128)S(1)} %get-tuple-element.162), channel_id=1, source_target_pairs={{0,16},{16,32},{32,48},{48,64},{64,80},{80,96},{96,112},{112,128},... | collective-permute-start | bytes 786440 | tf_op jit(solution)/shard_map/while/body/eval_jaxpr/ppermute | solution.py:10
  159.5 11.6 %collective-permute-start = (f32[256,256]{1,0:T(8,128)S(1)}, f32[256,256]{1,0:T(8,128)S(1)}, u32[]{:S(2)}, u32[]{:S(2)}) collective-permute-start(f32[256,256]{1,0:T(8,128)S(1)} %get-tuple-element.162), channel_id=1, source_target_pairs={{0,16},{16,32},{32,48},{48,64},{64,80},{80,96},{96,112},{112,128},... | collective-permute-start | bytes 786440 | tf_op jit(solution)/shard_map/while/body/eval_jaxpr/ppermute | solution.py:10
  171.1 11.6 %collective-permute-start = (f32[256,256]{1,0:T(8,128)S(1)}, f32[256,256]{1,0:T(8,128)S(1)}, u32[]{:S(2)}, u32[]{:S(2)}) collective-permute-start(f32[256,256]{1,0:T(8,128)S(1)} %get-tuple-element.162), channel_id=1, source_target_pairs={{0,16},{16,32},{32,48},{48,64},{64,80},{80,96},{96,112},{112,128},... | collective-permute-start | bytes 786440 | tf_op jit(solution)/shard_map/while/body/eval_jaxpr/ppermute | solution.py:10
  182.7 11.8 %collective-permute-start = (f32[256,256]{1,0:T(8,128)S(1)}, f32[256,256]{1,0:T(8,128)S(1)}, u32[]{:S(2)}, u32[]{:S(2)}) collective-permute-start(f32[256,256]{1,0:T(8,128)S(1)} %get-tuple-element.162), channel_id=1, source_target_pairs={{0,16},{16,32},{32,48},{48,64},{64,80},{80,96},{96,112},{112,128},... | collective-permute-start | bytes 786440 | tf_op jit(solution)/shard_map/while/body/eval_jaxpr/ppermute | solution.py:10
  194.4 12.8 %collective-permute-start = (f32[256,256]{1,0:T(8,128)S(1)}, f32[256,256]{1,0:T(8,128)S(1)}, u32[]{:S(2)}, u32[]{:S(2)}) collective-permute-start(f32[256,256]{1,0:T(8,128)S(1)} %get-tuple-element.162), channel_id=1, source_target_pairs={{0,16},{16,32},{32,48},{48,64},{64,80},{80,96},{96,112},{112,128},... | collective-permute-start | bytes 786440 | tf_op jit(solution)/shard_map/while/body/eval_jaxpr/ppermute | solution.py:10
  207.3 14.1 %collective-permute-start = (f32[256,256]{1,0:T(8,128)S(1)}, f32[256,256]{1,0:T(8,128)S(1)}, u32[]{:S(2)}, u32[]{:S(2)}) collective-permute-start(f32[256,256]{1,0:T(8,128)S(1)} %get-tuple-element.162), channel_id=1, source_target_pairs={{0,16},{16,32},{32,48},{48,64},{64,80},{80,96},{96,112},{112,128},... | collective-permute-start | bytes 786440 | tf_op jit(solution)/shard_map/while/body/eval_jaxpr/ppermute | solution.py:10
  221.3 13.5 %collective-permute-start = (f32[256,256]{1,0:T(8,128)S(1)}, f32[256,256]{1,0:T(8,128)S(1)}, u32[]{:S(2)}, u32[]{:S(2)}) collective-permute-start(f32[256,256]{1,0:T(8,128)S(1)} %get-tuple-element.162), channel_id=1, source_target_pairs={{0,16},{16,32},{32,48},{48,64},{64,80},{80,96},{96,112},{112,128},... | collective-permute-start | bytes 786440 | tf_op jit(solution)/shard_map/while/body/eval_jaxpr/ppermute | solution.py:10
  234.9 12.7 %collective-permute-start = (f32[256,256]{1,0:T(8,128)S(1)}, f32[256,256]{1,0:T(8,128)S(1)}, u32[]{:S(2)}, u32[]{:S(2)}) collective-permute-start(f32[256,256]{1,0:T(8,128)S(1)} %get-tuple-element.162), channel_id=1, source_target_pairs={{0,16},{16,32},{32,48},{48,64},{64,80},{80,96},{96,112},{112,128},... | collective-permute-start | bytes 786440 | tf_op jit(solution)/shard_map/while/body/eval_jaxpr/ppermute | solution.py:10
  247.6 11.8 %collective-permute-start = (f32[256,256]{1,0:T(8,128)S(1)}, f32[256,256]{1,0:T(8,128)S(1)}, u32[]{:S(2)}, u32[]{:S(2)}) collective-permute-start(f32[256,256]{1,0:T(8,128)S(1)} %get-tuple-element.162), channel_id=1, source_target_pairs={{0,16},{16,32},{32,48},{48,64},{64,80},{80,96},{96,112},{112,128},... | collective-permute-start | bytes 786440 | tf_op jit(solution)/shard_map/while/body/eval_jaxpr/ppermute | solution.py:10
  259.4 11.6 %collective-permute-start = (f32[256,256]{1,0:T(8,128)S(1)}, f32[256,256]{1,0:T(8,128)S(1)}, u32[]{:S(2)}, u32[]{:S(2)}) collective-permute-start(f32[256,256]{1,0:T(8,128)S(1)} %get-tuple-element.162), channel_id=1, source_target_pairs={{0,16},{16,32},{32,48},{48,64},{64,80},{80,96},{96,112},{112,128},... | collective-permute-start | bytes 786440 | tf_op jit(solution)/shard_map/while/body/eval_jaxpr/ppermute | solution.py:10
  271.0 11.6 %collective-permute-start = (f32[256,256]{1,0:T(8,128)S(1)}, f32[256,256]{1,0:T(8,128)S(1)}, u32[]{:S(2)}, u32[]{:S(2)}) collective-permute-start(f32[256,256]{1,0:T(8,128)S(1)} %get-tuple-element.162), channel_id=1, source_target_pairs={{0,16},{16,32},{32,48},{48,64},{64,80},{80,96},{96,112},{112,128},... | collective-permute-start | bytes 786440 | tf_op jit(solution)/shard_map/while/body/eval_jaxpr/ppermute | solution.py:10
  282.5 11.6 %collective-permute-start = (f32[256,256]{1,0:T(8,128)S(1)}, f32[256,256]{1,0:T(8,128)S(1)}, u32[]{:S(2)}, u32[]{:S(2)}) collective-permute-start(f32[256,256]{1,0:T(8,128)S(1)} %get-tuple-element.162), channel_id=1, source_target_pairs={{0,16},{16,32},{32,48},{48,64},{64,80},{80,96},{96,112},{112,128},... | collective-permute-start | bytes 786440 | tf_op jit(solution)/shard_map/while/body/eval_jaxpr/ppermute | solution.py:10
  294.9 11.6 %collective-permute-start = (f32[256,256]{1,0:T(8,128)S(1)}, f32[256,256]{1,0:T(8,128)S(1)}, u32[]{:S(2)}, u32[]{:S(2)}) collective-permute-start(f32[256,256]{1,0:T(8,128)S(1)} %get-tuple-element.162), channel_id=1, source_target_pairs={{0,16},{16,32},{32,48},{48,64},{64,80},{80,96},{96,112},{112,128},... | collective-permute-start | bytes 786440 | tf_op jit(solution)/shard_map/while/body/eval_jaxpr/ppermute | solution.py:10
  306.5 12.0 %collective-permute-start = (f32[256,256]{1,0:T(8,128)S(1)}, f32[256,256]{1,0:T(8,128)S(1)}, u32[]{:S(2)}, u32[]{:S(2)}) collective-permute-start(f32[256,256]{1,0:T(8,128)S(1)} %get-tuple-element.162), channel_id=1, source_target_pairs={{0,16},{16,32},{32,48},{48,64},{64,80},{80,96},{96,112},{112,128},... | collective-permute-start | bytes 786440 | tf_op jit(solution)/shard_map/while/body/eval_jaxpr/ppermute | solution.py:10
  318.5 13.1 %collective-permute-start = (f32[256,256]{1,0:T(8,128)S(1)}, f32[256,256]{1,0:T(8,128)S(1)}, u32[]{:S(2)}, u32[]{:S(2)}) collective-permute-start(f32[256,256]{1,0:T(8,128)S(1)} %get-tuple-element.162), channel_id=1, source_target_pairs={{0,16},{16,32},{32,48},{48,64},{64,80},{80,96},{96,112},{112,128},... | collective-permute-start | bytes 786440 | tf_op jit(solution)/shard_map/while/body/eval_jaxpr/ppermute | solution.py:10
  331.6 14.3 %collective-permute-start = (f32[256,256]{1,0:T(8,128)S(1)}, f32[256,256]{1,0:T(8,128)S(1)}, u32[]{:S(2)}, u32[]{:S(2)}) collective-permute-start(f32[256,256]{1,0:T(8,128)S(1)} %get-tuple-element.162), channel_id=1, source_target_pairs={{0,16},{16,32},{32,48},{48,64},{64,80},{80,96},{96,112},{112,128},... | collective-permute-start | bytes 786440 | tf_op jit(solution)/shard_map/while/body/eval_jaxpr/ppermute | solution.py:10
  345.9 13.5 %collective-permute-start = (f32[256,256]{1,0:T(8,128)S(1)}, f32[256,256]{1,0:T(8,128)S(1)}, u32[]{:S(2)}, u32[]{:S(2)}) collective-permute-start(f32[256,256]{1,0:T(8,128)S(1)} %get-tuple-element.162), channel_id=1, source_target_pairs={{0,16},{16,32},{32,48},{48,64},{64,80},{80,96},{96,112},{112,128},... | collective-permute-start | bytes 786440 | tf_op jit(solution)/shard_map/while/body/eval_jaxpr/ppermute | solution.py:10
  359.4 12.7 %collective-permute-start = (f32[256,256]{1,0:T(8,128)S(1)}, f32[256,256]{1,0:T(8,128)S(1)}, u32[]{:S(2)}, u32[]{:S(2)}) collective-permute-start(f32[256,256]{1,0:T(8,128)S(1)} %get-tuple-element.162), channel_id=1, source_target_pairs={{0,16},{16,32},{32,48},{48,64},{64,80},{80,96},{96,112},{112,128},... | collective-permute-start | bytes 786440 | tf_op jit(solution)/shard_map/while/body/eval_jaxpr/ppermute | solution.py:10
  372.1 11.8 %collective-permute-start = (f32[256,256]{1,0:T(8,128)S(1)}, f32[256,256]{1,0:T(8,128)S(1)}, u32[]{:S(2)}, u32[]{:S(2)}) collective-permute-start(f32[256,256]{1,0:T(8,128)S(1)} %get-tuple-element.162), channel_id=1, source_target_pairs={{0,16},{16,32},{32,48},{48,64},{64,80},{80,96},{96,112},{112,128},... | collective-permute-start | bytes 786440 | tf_op jit(solution)/shard_map/while/body/eval_jaxpr/ppermute | solution.py:10
  383.9 11.6 %collective-permute-start = (f32[256,256]{1,0:T(8,128)S(1)}, f32[256,256]{1,0:T(8,128)S(1)}, u32[]{:S(2)}, u32[]{:S(2)}) collective-permute-start(f32[256,256]{1,0:T(8,128)S(1)} %get-tuple-element.162), channel_id=1, source_target_pairs={{0,16},{16,32},{32,48},{48,64},{64,80},{80,96},{96,112},{112,128},... | collective-permute-start | bytes 786440 | tf_op jit(solution)/shard_map/while/body/eval_jaxpr/ppermute | solution.py:10
  395.5 11.6 %collective-permute-start = (f32[256,256]{1,0:T(8,128)S(1)}, f32[256,256]{1,0:T(8,128)S(1)}, u32[]{:S(2)}, u32[]{:S(2)}) collective-permute-start(f32[256,256]{1,0:T(8,128)S(1)} %get-tuple-element.162), channel_id=1, source_target_pairs={{0,16},{16,32},{32,48},{48,64},{64,80},{80,96},{96,112},{112,128},... | collective-permute-start | bytes 786440 | tf_op jit(solution)/shard_map/while/body/eval_jaxpr/ppermute | solution.py:10
  407.0 11.6 %collective-permute-start = (f32[256,256]{1,0:T(8,128)S(1)}, f32[256,256]{1,0:T(8,128)S(1)}, u32[]{:S(2)}, u32[]{:S(2)}) collective-permute-start(f32[256,256]{1,0:T(8,128)S(1)} %get-tuple-element.162), channel_id=1, source_target_pairs={{0,16},{16,32},{32,48},{48,64},{64,80},{80,96},{96,112},{112,128},... | collective-permute-start | bytes 786440 | tf_op jit(solution)/shard_map/while/body/eval_jaxpr/ppermute | solution.py:10
  418.6 11.6 %collective-permute-start = (f32[256,256]{1,0:T(8,128)S(1)}, f32[256,256]{1,0:T(8,128)S(1)}, u32[]{:S(2)}, u32[]{:S(2)}) collective-permute-start(f32[256,256]{1,0:T(8,128)S(1)} %get-tuple-element.162), channel_id=1, source_target_pairs={{0,16},{16,32},{32,48},{48,64},{64,80},{80,96},{96,112},{112,128},... | collective-permute-start | bytes 786440 | tf_op jit(solution)/shard_map/while/body/eval_jaxpr/ppermute | solution.py:10
  430.2 12.0 %collective-permute-start = (f32[256,256]{1,0:T(8,128)S(1)}, f32[256,256]{1,0:T(8,128)S(1)}, u32[]{:S(2)}, u32[]{:S(2)}) collective-permute-start(f32[256,256]{1,0:T(8,128)S(1)} %get-tuple-element.162), channel_id=1, source_target_pairs={{0,16},{16,32},{32,48},{48,64},{64,80},{80,96},{96,112},{112,128},... | collective-permute-start | bytes 786440 | tf_op jit(solution)/shard_map/while/body/eval_jaxpr/ppermute | solution.py:10
  442.2 11.6 %collective-permute-start = (f32[256,256]{1,0:T(8,128)S(1)}, f32[256,256]{1,0:T(8,128)S(1)}, u32[]{:S(2)}, u32[]{:S(2)}) collective-permute-start(f32[256,256]{1,0:T(8,128)S(1)} %get-tuple-element.162), channel_id=1, source_target_pairs={{0,16},{16,32},{32,48},{48,64},{64,80},{80,96},{96,112},{112,128},... | collective-permute-start | bytes 786440 | tf_op jit(solution)/shard_map/while/body/eval_jaxpr/ppermute | solution.py:10
  453.8 11.6 %collective-permute-start = (f32[256,256]{1,0:T(8,128)S(1)}, f32[256,256]{1,0:T(8,128)S(1)}, u32[]{:S(2)}, u32[]{:S(2)}) collective-permute-start(f32[256,256]{1,0:T(8,128)S(1)} %get-tuple-element.162), channel_id=1, source_target_pairs={{0,16},{16,32},{32,48},{48,64},{64,80},{80,96},{96,112},{112,128},... | collective-permute-start | bytes 786440 | tf_op jit(solution)/shard_map/while/body/eval_jaxpr/ppermute | solution.py:10
  465.4 11.6 %collective-permute-start = (f32[256,256]{1,0:T(8,128)S(1)}, f32[256,256]{1,0:T(8,128)S(1)}, u32[]{:S(2)}, u32[]{:S(2)}) collective-permute-start(f32[256,256]{1,0:T(8,128)S(1)} %get-tuple-element.162), channel_id=1, source_target_pairs={{0,16},{16,32},{32,48},{48,64},{64,80},{80,96},{96,112},{112,128},... | collective-permute-start | bytes 786440 | tf_op jit(solution)/shard_map/while/body/eval_jaxpr/ppermute | solution.py:10
  476.9 0.7 copy-start.1
Sparse Core Ops, SparseCore 0:
  10.9 46.2 all-gather.1
where the time goes:
time: 486 us; the launch traced here: 484 us
  waiting for transfers between devices  364 us (75%)
  starting transfers between devices  60.7 us (12%)
  blocking collectives  33.1 us (7%)
  between operations  14.1 us (3%)
  matrix products  10.7 us (2%)
    ppermute x31, waiting for transfers between devices, passed_along(): return lax.ppermute(x, axis, pairs)  317 us
    ppermute x31, starting transfers between devices, passed_along(): return lax.ppermute(x, axis, pairs)  60.6 us
    all_gather x1, waiting for transfers between devices, body(): lax.all_gather(picked_one, 'blk', axis=0, tiled=True)  46.4 us
    all_gather x1, blocking collectives, body(): lax.all_gather(picked_two, 'blk', axis=0, tiled=True)  18 us
    all_gather x1, blocking collectives, body(): lax.all_gather(edge_rows, 'blk', axis=0, tiled=True).astype(jnp.float32)  15.1 us
  transfers between devices with their start and end apart: 32, of which 32 were waited for; matrix products, arithmetic and copies ran while one was open for 0% of the time, Pallas kernels for 0%

commit v1 on v0

--- a/solution.py
+++ b/solution.py
@@ -2,6 +2,11 @@
 import jax.numpy as jnp
 from jax import lax
 from jax.sharding import PartitionSpec as P
+
+
+def swapped_in(value, axis, along):
+    stack = jnp.stack([value] * lax.axis_size(axis))
+    return jnp.concatenate(lax.all_to_all(stack, axis, 0, 0), axis=along)
 
 
 def passed_along(x, axis, by):
@@ -39,11 +44,7 @@
     columns = factor_one
     updated = (
         strip_block[:, panel_width:].astype(jnp.float32)
-        - jnp.dot(
-            columns,
-            lax.all_gather(picked_one, "blk", axis=0, tiled=True),
-            preferred_element_type=jnp.float32,
-        )
+        - jnp.dot(columns, swapped_in(picked_one, "blk", 0), preferred_element_type=jnp.float32)
     ).astype(jnp.bfloat16)
     factor_two = jnp.dot(
         updated[:, :panel_width], inverse_pair[1], preferred_element_type=jnp.float32

time: 486 us -> 463 us (0.953)
  waiting for transfers between devices: 364 us -> 344 us
  between operations: 14.1 us -> 0.68 us
  starting transfers between devices: 60.7 us -> 71.1 us
    all_gather x1 -> x0, waiting for transfers between devices: 46.4 us -> none  [body(): lax.all_gather(picked_one, 'blk', axis=0, tiled=True)]
    all_to_all x0 -> x1, waiting for transfers between devices: none -> 26.7 us  [swapped_in(): return jnp.concatenate(lax.all_to_all(stack, axis, 0, 0), axis=along)]
    all_to_all x0 -> x1, starting transfers between devices: none -> 10.4 us  [swapped_in(): return jnp.concatenate(lax.all_to_all(stack, axis, 0, 0), axis=along)]
where the time goes in v1:
time: 463 us; the launch traced here: 462 us
  waiting for transfers between devices  344 us (74%)
  starting transfers between devices  71.1 us (15%)
  blocking collectives  33.6 us (7%)
  matrix products  9.74 us (2%)
    ppermute x31, waiting for transfers between devices, passed_along(): return lax.ppermute(x, axis, pairs)  317 us
    ppermute x31, starting transfers between devices, passed_along(): return lax.ppermute(x, axis, pairs)  60.7 us
    all_to_all x1, waiting for transfers between devices, swapped_in(): return jnp.concatenate(lax.all_to_all(stack, axis, 0, 0), axis=along)  26.7 us
    all_gather x1, blocking collectives, body(): lax.all_gather(picked_two, 'blk', axis=0, tiled=True)  18.3 us
    all_gather x1, blocking collectives, body(): lax.all_gather(edge_rows, 'blk', axis=0, tiled=True).astype(jnp.float32)  15.3 us
    all_to_all x1, starting transfers between devices, swapped_in(): return jnp.concatenate(lax.all_to_all(stack, axis, 0, 0), axis=along)  10.4 us
  transfers between devices with their start and end apart: 32, of which 32 were waited for; matrix products, arithmetic and copies ran while one was open for 0% of the time, Pallas kernels for 0%

profile of v1, /device:TPU:32, one launch (start us, length us, event | category | flops | bytes accessed | tf_op | source)
XLA Modules:
  0.0 462.3 jit_solution(17182475341930651778)
XLA Ops:
  1.5 2.0 convolution_convert_fusion.1
  4.6 10.4 %all-to-all-start = ((bf16[16,16,2048]{2,1,0:T(8,128)(2,1)}), bf16[16,16,2048]{2,1,0:T(8,128)(2,1)S(1)}, u32[]{:S(2)}, u32[]{:S(2)}) async-start(bf16[16,16,2048]{2,1,0:T(8,128)(2,1)} %stack.2), calls=%async_computation | async-start | bytes 2097152 | tf_op jit(solution)/shard_map/all_to_all | solution.py:9
  15.0 26.7 %all-to-all-done = bf16[16,16,2048]{2,1,0:T(8,128)(2,1)S(1)} async-done(((bf16[16,16,2048]{2,1,0:T(8,128)(2,1)}), bf16[16,16,2048]{2,1,0:T(8,128)(2,1)S(1)}, u32[]{:S(2)}, u32[]{:S(2)}) %all-to-all-start) | async-done | bytes 1048608 | tf_op jit(solution)/shard_map/all_to_all | solution.py:9
  41.6 2.5 subtract_convert_fusion
  44.5 18.3 %all_gather.6 = bf16[256,1792]{1,0:T(8,128)(2,1)S(1)} all-gather(bf16[16,1792]{1,0:T(8,128)(2,1)S(1)} %convolution_convert_fusion), channel_id=1, replica_groups=mesh['tm'=32,'blk'=16] {'blk'}, dimensions={0}, use_global_device_ids=true | all-gather | bytes 974848 | tf_op jit(solution)/shard_map/all_gather | solution.py:60
  62.9 3.0 subtract_convert_fusion.1
  66.9 15.3 %all_gather.7 = bf16[256,256]{1,0:T(8,128)(2,1)S(1)} all-gather(bf16[16,256]{1,0:T(8,128)(2,1)S(1)} %convolution_convert_fusion.4), channel_id=1, replica_groups=mesh['tm'=32,'blk'=16] {'blk'}, dimensions={0}, use_global_device_ids=true | all-gather | bytes 139264 | tf_op jit(solution)/shard_map/all_gather | solution.py:67
  82.3 379.3 %while.16 = (s32[]{:T(128)}, f32[256,256]{1,0:T(8,128)S(1)}, s32[]{:T(128)}, f32[256,256]{1,0:T(8,128)S(1)}, f32[256,256]{1,0:T(8,128)S(1)}, /*index=5*/s32[]{:T(128)}) while((s32[]{:T(128)}, f32[256,256]{1,0:T(8,128)S(1)}, s32[]{:T(128)}, f32[256,256]{1,0:T(8,128)S(1)}, f32[256,256]{1,0:T(8,128)S(1)}, /*index=5*/s32[]{:T(128)}) %tuple.49), condition=%wide.region_3.0_spmd, body=%wide.region_0.0_spmd.sunk | while | flops 402718720 | bytes 2883739 | solution.py:83
  82.3 3.4 collective-permute-start
  85.7 10.4 %collective-permute-done = f32[256,256]{1,0:T(8,128)S(1)} collective-permute-done((f32[256,256]{1,0:T(8,128)S(1)}, f32[256,256]{1,0:T(8,128)S(1)}, u32[]{:S(2)}, u32[]{:S(2)}) %collective-permute-start) | collective-permute-done | bytes 262176 | tf_op jit(solution)/shard_map/while/body/eval_jaxpr/ppermute | solution.py:15
  96.0 1.9 collective-permute-start
  98.0 11.0 %collective-permute-done = f32[256,256]{1,0:T(8,128)S(1)} collective-permute-done((f32[256,256]{1,0:T(8,128)S(1)}, f32[256,256]{1,0:T(8,128)S(1)}, u32[]{:S(2)}, u32[]{:S(2)}) %collective-permute-start) | collective-permute-done | bytes 262176 | tf_op jit(solution)/shard_map/while/body/eval_jaxpr/ppermute | solution.py:15
  109.0 1.9 collective-permute-start
  110.9 10.1 %collective-permute-done = f32[256,256]{1,0:T(8,128)S(1)} collective-permute-done((f32[256,256]{1,0:T(8,128)S(1)}, f32[256,256]{1,0:T(8,128)S(1)}, u32[]{:S(2)}, u32[]{:S(2)}) %collective-permute-start) | collective-permute-done | bytes 262176 | tf_op jit(solution)/shard_map/while/body/eval_jaxpr/ppermute | solution.py:15
  121.0 1.9 collective-permute-start
  122.9 9.7 %collective-permute-done = f32[256,256]{1,0:T(8,128)S(1)} collective-permute-done((f32[256,256]{1,0:T(8,128)S(1)}, f32[256,256]{1,0:T(8,128)S(1)}, u32[]{:S(2)}, u32[]{:S(2)}) %collective-permute-start) | collective-permute-done | bytes 262176 | tf_op jit(solution)/shard_map/while/body/eval_jaxpr/ppermute | solution.py:15
  132.6 1.9 collective-permute-start
  134.5 9.7 %collective-permute-done = f32[256,256]{1,0:T(8,128)S(1)} collective-permute-done((f32[256,256]{1,0:T(8,128)S(1)}, f32[256,256]{1,0:T(8,128)S(1)}, u32[]{:S(2)}, u32[]{:S(2)}) %collective-permute-start) | collective-permute-done | bytes 262176 | tf_op jit(solution)/shard_map/while/body/eval_jaxpr/ppermute | solution.py:15
  144.2 1.9 collective-permute-start
  146.1 9.7 %collective-permute-done = f32[256,256]{1,0:T(8,128)S(1)} collective-permute-done((f32[256,256]{1,0:T(8,128)S(1)}, f32[256,256]{1,0:T(8,128)S(1)}, u32[]{:S(2)}, u32[]{:S(2)}) %collective-permute-start) | collective-permute-done | bytes 262176 | tf_op jit(solution)/shard_map/while/body/eval_jaxpr/ppermute | solution.py:15
  155.7 1.9 collective-permute-start
  157.7 9.7 %collective-permute-done = f32[256,256]{1,0:T(8,128)S(1)} collective-permute-done((f32[256,256]{1,0:T(8,128)S(1)}, f32[256,256]{1,0:T(8,128)S(1)}, u32[]{:S(2)}, u32[]{:S(2)}) %collective-permute-start) | collective-permute-done | bytes 262176 | tf_op jit(solution)/shard_map/while/body/eval_jaxpr/ppermute | solution.py:15
  167.3 1.9 collective-permute-start
  169.2 9.8 %collective-permute-done = f32[256,256]{1,0:T(8,128)S(1)} collective-permute-done((f32[256,256]{1,0:T(8,128)S(1)}, f32[256,256]{1,0:T(8,128)S(1)}, u32[]{:S(2)}, u32[]{:S(2)}) %collective-permute-start) | collective-permute-done | bytes 262176 | tf_op jit(solution)/shard_map/while/body/eval_jaxpr/ppermute | solution.py:15
  179.1 1.9 collective-permute-start
  181.0 10.9 %collective-permute-done = f32[256,256]{1,0:T(8,128)S(1)} collective-permute-done((f32[256,256]{1,0:T(8,128)S(1)}, f32[256,256]{1,0:T(8,128)S(1)}, u32[]{:S(2)}, u32[]{:S(2)}) %collective-permute-start) | collective-permute-done | bytes 262176 | tf_op jit(solution)/shard_map/while/body/eval_jaxpr/ppermute | solution.py:15
  191.9 1.9 collective-permute-start
  193.8 12.1 %collective-permute-done = f32[256,256]{1,0:T(8,128)S(1)} collective-permute-done((f32[256,256]{1,0:T(8,128)S(1)}, f32[256,256]{1,0:T(8,128)S(1)}, u32[]{:S(2)}, u32[]{:S(2)}) %collective-permute-start) | collective-permute-done | bytes 262176 | tf_op jit(solution)/shard_map/while/body/eval_jaxpr/ppermute | solution.py:15
  206.0 1.9 collective-permute-start
  207.9 11.6 %collective-permute-done = f32[256,256]{1,0:T(8,128)S(1)} collective-permute-done((f32[256,256]{1,0:T(8,128)S(1)}, f32[256,256]{1,0:T(8,128)S(1)}, u32[]{:S(2)}, u32[]{:S(2)}) %collective-permute-start) | collective-permute-done | bytes 262176 | tf_op jit(solution)/shard_map/while/body/eval_jaxpr/ppermute | solution.py:15
  219.5 1.9 collective-permute-start
  221.5 10.8 %collective-permute-done = f32[256,256]{1,0:T(8,128)S(1)} collective-permute-done((f32[256,256]{1,0:T(8,128)S(1)}, f32[256,256]{1,0:T(8,128)S(1)}, u32[]{:S(2)}, u32[]{:S(2)}) %collective-permute-start) | collective-permute-done | bytes 262176 | tf_op jit(solution)/shard_map/while/body/eval_jaxpr/ppermute | solution.py:15
  232.3 1.9 collective-permute-start
  234.2 9.9 %collective-permute-done = f32[256,256]{1,0:T(8,128)S(1)} collective-permute-done((f32[256,256]{1,0:T(8,128)S(1)}, f32[256,256]{1,0:T(8,128)S(1)}, u32[]{:S(2)}, u32[]{:S(2)}) %collective-permute-start) | collective-permute-done | bytes 262176 | tf_op jit(solution)/shard_map/while/body/eval_jaxpr/ppermute | solution.py:15
  244.0 1.9 collective-permute-start
  246.0 9.7 %collective-permute-done = f32[256,256]{1,0:T(8,128)S(1)} collective-permute-done((f32[256,256]{1,0:T(8,128)S(1)}, f32[256,256]{1,0:T(8,128)S(1)}, u32[]{:S(2)}, u32[]{:S(2)}) %collective-permute-start) | collective-permute-done | bytes 262176 | tf_op jit(solution)/shard_map/while/body/eval_jaxpr/ppermute | solution.py:15
  255.6 1.9 collective-permute-start
  257.5 9.7 %collective-permute-done = f32[256,256]{1,0:T(8,128)S(1)} collective-permute-done((f32[256,256]{1,0:T(8,128)S(1)}, f32[256,256]{1,0:T(8,128)S(1)}, u32[]{:S(2)}, u32[]{:S(2)}) %collective-permute-start) | collective-permute-done | bytes 262176 | tf_op jit(solution)/shard_map/while/body/eval_jaxpr/ppermute | solution.py:15
  267.2 1.9 collective-permute-start
  269.1 9.7 %collective-permute-done = f32[256,256]{1,0:T(8,128)S(1)} collective-permute-done((f32[256,256]{1,0:T(8,128)S(1)}, f32[256,256]{1,0:T(8,128)S(1)}, u32[]{:S(2)}, u32[]{:S(2)}) %collective-permute-start) | collective-permute-done | bytes 262176 | tf_op jit(solution)/shard_map/while/body/eval_jaxpr/ppermute | solution.py:15
  279.6 1.9 collective-permute-start
  281.5 9.7 %collective-permute-done = f32[256,256]{1,0:T(8,128)S(1)} collective-permute-done((f32[256,256]{1,0:T(8,128)S(1)}, f32[256,256]{1,0:T(8,128)S(1)}, u32[]{:S(2)}, u32[]{:S(2)}) %collective-permute-start) | collective-permute-done | bytes 262176 | tf_op jit(solution)/shard_map/while/body/eval_jaxpr/ppermute | solution.py:15
  291.2 1.9 collective-permute-start
  293.1 10.1 %collective-permute-done = f32[256,256]{1,0:T(8,128)S(1)} collective-permute-done((f32[256,256]{1,0:T(8,128)S(1)}, f32[256,256]{1,0:T(8,128)S(1)}, u32[]{:S(2)}, u32[]{:S(2)}) %collective-permute-start) | collective-permute-done | bytes 262176 | tf_op jit(solution)/shard_map/while/body/eval_jaxpr/ppermute | solution.py:15
  303.2 1.9 collective-permute-start
  305.1 11.2 %collective-permute-done = f32[256,256]{1,0:T(8,128)S(1)} collective-permute-done((f32[256,256]{1,0:T(8,128)S(1)}, f32[256,256]{1,0:T(8,128)S(1)}, u32[]{:S(2)}, u32[]{:S(2)}) %collective-permute-start) | collective-permute-done | bytes 262176 | tf_op jit(solution)/shard_map/while/body/eval_jaxpr/ppermute | solution.py:15
  316.3 1.9 collective-permute-start
  318.2 12.3 %collective-permute-done = f32[256,256]{1,0:T(8,128)S(1)} collective-permute-done((f32[256,256]{1,0:T(8,128)S(1)}, f32[256,256]{1,0:T(8,128)S(1)}, u32[]{:S(2)}, u32[]{:S(2)}) %collective-permute-start) | collective-permute-done | bytes 262176 | tf_op jit(solution)/shard_map/while/body/eval_jaxpr/ppermute | solution.py:15
  330.5 1.9 collective-permute-start
  332.5 11.6 %collective-permute-done = f32[256,256]{1,0:T(8,128)S(1)} collective-permute-done((f32[256,256]{1,0:T(8,128)S(1)}, f32[256,256]{1,0:T(8,128)S(1)}, u32[]{:S(2)}, u32[]{:S(2)}) %collective-permute-start) | collective-permute-done | bytes 262176 | tf_op jit(solution)/shard_map/while/body/eval_jaxpr/ppermute | solution.py:15
  344.1 1.9 collective-permute-start
  346.0 10.8 %collective-permute-done = f32[256,256]{1,0:T(8,128)S(1)} collective-permute-done((f32[256,256]{1,0:T(8,128)S(1)}, f32[256,256]{1,0:T(8,128)S(1)}, u32[]{:S(2)}, u32[]{:S(2)}) %collective-permute-start) | collective-permute-done | bytes 262176 | tf_op jit(solution)/shard_map/while/body/eval_jaxpr/ppermute | solution.py:15
  356.8 1.9 collective-permute-start
  358.7 9.8 %collective-permute-done = f32[256,256]{1,0:T(8,128)S(1)} collective-permute-done((f32[256,256]{1,0:T(8,128)S(1)}, f32[256,256]{1,0:T(8,128)S(1)}, u32[]{:S(2)}, u32[]{:S(2)}) %collective-permute-start) | collective-permute-done | bytes 262176 | tf_op jit(solution)/shard_map/while/body/eval_jaxpr/ppermute | solution.py:15
  368.5 1.9 collective-permute-start
  370.5 9.7 %collective-permute-done = f32[256,256]{1,0:T(8,128)S(1)} collective-permute-done((f32[256,256]{1,0:T(8,128)S(1)}, f32[256,256]{1,0:T(8,128)S(1)}, u32[]{:S(2)}, u32[]{:S(2)}) %collective-permute-start) | collective-permute-done | bytes 262176 | tf_op jit(solution)/shard_map/while/body/eval_jaxpr/ppermute | solution.py:15
  380.1 1.9 collective-permute-start
  382.0 9.7 %collective-permute-done = f32[256,256]{1,0:T(8,128)S(1)} collective-permute-done((f32[256,256]{1,0:T(8,128)S(1)}, f32[256,256]{1,0:T(8,128)S(1)}, u32[]{:S(2)}, u32[]{:S(2)}) %collective-permute-start) | collective-permute-done | bytes 262176 | tf_op jit(solution)/shard_map/while/body/eval_jaxpr/ppermute | solution.py:15
  393.6 9.7 %collective-permute-done = f32[256,256]{1,0:T(8,128)S(1)} collective-permute-done((f32[256,256]{1,0:T(8,128)S(1)}, f32[256,256]{1,0:T(8,128)S(1)}, u32[]{:S(2)}, u32[]{:S(2)}) %collective-permute-start) | collective-permute-done | bytes 262176 | tf_op jit(solution)/shard_map/while/body/eval_jaxpr/ppermute | solution.py:15
  405.2 9.7 %collective-permute-done = f32[256,256]{1,0:T(8,128)S(1)} collective-permute-done((f32[256,256]{1,0:T(8,128)S(1)}, f32[256,256]{1,0:T(8,128)S(1)}, u32[]{:S(2)}, u32[]{:S(2)}) %collective-permute-start) | collective-permute-done | bytes 262176 | tf_op jit(solution)/shard_map/while/body/eval_jaxpr/ppermute | solution.py:15
  416.8 10.1 %collective-permute-done = f32[256,256]{1,0:T(8,128)S(1)} collective-permute-done((f32[256,256]{1,0:T(8,128)S(1)}, f32[256,256]{1,0:T(8,128)S(1)}, u32[]{:S(2)}, u32[]{:S(2)}) %collective-permute-start) | collective-permute-done | bytes 262176 | tf_op jit(solution)/shard_map/while/body/eval_jaxpr/ppermute | solution.py:15
  428.8 9.7 %collective-permute-done = f32[256,256]{1,0:T(8,128)S(1)} collective-permute-done((f32[256,256]{1,0:T(8,128)S(1)}, f32[256,256]{1,0:T(8,128)S(1)}, u32[]{:S(2)}, u32[]{:S(2)}) %collective-permute-start) | collective-permute-done | bytes 262176 | tf_op jit(solution)/shard_map/while/body/eval_jaxpr/ppermute | solution.py:15
  440.4 9.7 %collective-permute-done = f32[256,256]{1,0:T(8,128)S(1)} collective-permute-done((f32[256,256]{1,0:T(8,128)S(1)}, f32[256,256]{1,0:T(8,128)S(1)}, u32[]{:S(2)}, u32[]{:S(2)}) %collective-permute-start) | collective-permute-done | bytes 262176 | tf_op jit(solution)/shard_map/while/body/eval_jaxpr/ppermute | solution.py:15
  451.9 9.7 %collective-permute-done = f32[256,256]{1,0:T(8,128)S(1)} collective-permute-done((f32[256,256]{1,0:T(8,128)S(1)}, f32[256,256]{1,0:T(8,128)S(1)}, u32[]{:S(2)}, u32[]{:S(2)}) %collective-permute-start) | collective-permute-done | bytes 262176 | tf_op jit(solution)/shard_map/while/body/eval_jaxpr/ppermute | solution.py:15
  (52 shorter events, 17.2 us)
Async XLA Ops:
  3.5 38.2 %copy-start.2 = (bf16[1,2,256,256]{3,2,1,0:T(8,128)(2,1)S(1)}, bf16[1,2,256,256]{3,2,1,0:T(8,128)(2,1)}, u32[]{:S(2)}) copy-start(bf16[1,2,256,256]{3,2,1,0:T(8,128)(2,1)} %param.9) | copy-start | bytes 786436
  4.6 37.1 %all-to-all-start = ((bf16[16,16,2048]{2,1,0:T(8,128)(2,1)}), bf16[16,16,2048]{2,1,0:T(8,128)(2,1)S(1)}, u32[]{:S(2)}, u32[]{:S(2)}) async-start(bf16[16,16,2048]{2,1,0:T(8,128)(2,1)} %stack.2), calls=%async_computation | async-start | bytes 2097152 | tf_op jit(solution)/shard_map/all_to_all | solution.py:9
  62.8 19.4 %copy-start = (f32[1,256,256]{2,1,0:T(8,128)S(1)}, f32[1,256,256]{2,1,0:T(8,128)}, u32[]{:S(2)}) copy-start(f32[1,256,256]{2,1,0:T(8,128)} %param.10) | copy-start | bytes 786436
  82.3 13.8 %collective-permute-start = (f32[256,256]{1,0:T(8,128)S(1)}, f32[256,256]{1,0:T(8,128)S(1)}, u32[]{:S(2)}, u32[]{:S(2)}) collective-permute-start(f32[256,256]{1,0:T(8,128)S(1)} %get-tuple-element.162), channel_id=1, source_target_pairs={{0,16},{16,32},{32,48},{48,64},{64,80},{80,96},{96,112},{112,128},... | collective-permute-start | bytes 786440 | tf_op jit(solution)/shard_map/while/body/eval_jaxpr/ppermute | solution.py:15
  96.0 13.0 %collective-permute-start = (f32[256,256]{1,0:T(8,128)S(1)}, f32[256,256]{1,0:T(8,128)S(1)}, u32[]{:S(2)}, u32[]{:S(2)}) collective-permute-start(f32[256,256]{1,0:T(8,128)S(1)} %get-tuple-element.162), channel_id=1, source_target_pairs={{0,16},{16,32},{32,48},{48,64},{64,80},{80,96},{96,112},{112,128},... | collective-permute-start | bytes 786440 | tf_op jit(solution)/shard_map/while/body/eval_jaxpr/ppermute | solution.py:15
  109.0 12.0 %collective-permute-start = (f32[256,256]{1,0:T(8,128)S(1)}, f32[256,256]{1,0:T(8,128)S(1)}, u32[]{:S(2)}, u32[]{:S(2)}) collective-permute-start(f32[256,256]{1,0:T(8,128)S(1)} %get-tuple-element.162), channel_id=1, source_target_pairs={{0,16},{16,32},{32,48},{48,64},{64,80},{80,96},{96,112},{112,128},... | collective-permute-start | bytes 786440 | tf_op jit(solution)/shard_map/while/body/eval_jaxpr/ppermute | solution.py:15
  121.0 11.6 %collective-permute-start = (f32[256,256]{1,0:T(8,128)S(1)}, f32[256,256]{1,0:T(8,128)S(1)}, u32[]{:S(2)}, u32[]{:S(2)}) collective-permute-start(f32[256,256]{1,0:T(8,128)S(1)} %get-tuple-element.162), channel_id=1, source_target_pairs={{0,16},{16,32},{32,48},{48,64},{64,80},{80,96},{96,112},{112,128},... | collective-permute-start | bytes 786440 | tf_op jit(solution)/shard_map/while/body/eval_jaxpr/ppermute | solution.py:15
  132.6 11.6 %collective-permute-start = (f32[256,256]{1,0:T(8,128)S(1)}, f32[256,256]{1,0:T(8,128)S(1)}, u32[]{:S(2)}, u32[]{:S(2)}) collective-permute-start(f32[256,256]{1,0:T(8,128)S(1)} %get-tuple-element.162), channel_id=1, source_target_pairs={{0,16},{16,32},{32,48},{48,64},{64,80},{80,96},{96,112},{112,128},... | collective-permute-start | bytes 786440 | tf_op jit(solution)/shard_map/while/body/eval_jaxpr/ppermute | solution.py:15
  144.2 11.6 %collective-permute-start = (f32[256,256]{1,0:T(8,128)S(1)}, f32[256,256]{1,0:T(8,128)S(1)}, u32[]{:S(2)}, u32[]{:S(2)}) collective-permute-start(f32[256,256]{1,0:T(8,128)S(1)} %get-tuple-element.162), channel_id=1, source_target_pairs={{0,16},{16,32},{32,48},{48,64},{64,80},{80,96},{96,112},{112,128},... | collective-permute-start | bytes 786440 | tf_op jit(solution)/shard_map/while/body/eval_jaxpr/ppermute | solution.py:15
  155.7 11.6 %collective-permute-start = (f32[256,256]{1,0:T(8,128)S(1)}, f32[256,256]{1,0:T(8,128)S(1)}, u32[]{:S(2)}, u32[]{:S(2)}) collective-permute-start(f32[256,256]{1,0:T(8,128)S(1)} %get-tuple-element.162), channel_id=1, source_target_pairs={{0,16},{16,32},{32,48},{48,64},{64,80},{80,96},{96,112},{112,128},... | collective-permute-start | bytes 786440 | tf_op jit(solution)/shard_map/while/body/eval_jaxpr/ppermute | solution.py:15
  167.3 11.8 %collective-permute-start = (f32[256,256]{1,0:T(8,128)S(1)}, f32[256,256]{1,0:T(8,128)S(1)}, u32[]{:S(2)}, u32[]{:S(2)}) collective-permute-start(f32[256,256]{1,0:T(8,128)S(1)} %get-tuple-element.162), channel_id=1, source_target_pairs={{0,16},{16,32},{32,48},{48,64},{64,80},{80,96},{96,112},{112,128},... | collective-permute-start | bytes 786440 | tf_op jit(solution)/shard_map/while/body/eval_jaxpr/ppermute | solution.py:15
  179.1 12.8 %collective-permute-start = (f32[256,256]{1,0:T(8,128)S(1)}, f32[256,256]{1,0:T(8,128)S(1)}, u32[]{:S(2)}, u32[]{:S(2)}) collective-permute-start(f32[256,256]{1,0:T(8,128)S(1)} %get-tuple-element.162), channel_id=1, source_target_pairs={{0,16},{16,32},{32,48},{48,64},{64,80},{80,96},{96,112},{112,128},... | collective-permute-start | bytes 786440 | tf_op jit(solution)/shard_map/while/body/eval_jaxpr/ppermute | solution.py:15
  191.9 14.1 %collective-permute-start = (f32[256,256]{1,0:T(8,128)S(1)}, f32[256,256]{1,0:T(8,128)S(1)}, u32[]{:S(2)}, u32[]{:S(2)}) collective-permute-start(f32[256,256]{1,0:T(8,128)S(1)} %get-tuple-element.162), channel_id=1, source_target_pairs={{0,16},{16,32},{32,48},{48,64},{64,80},{80,96},{96,112},{112,128},... | collective-permute-start | bytes 786440 | tf_op jit(solution)/shard_map/while/body/eval_jaxpr/ppermute | solution.py:15
  206.0 13.5 %collective-permute-start = (f32[256,256]{1,0:T(8,128)S(1)}, f32[256,256]{1,0:T(8,128)S(1)}, u32[]{:S(2)}, u32[]{:S(2)}) collective-permute-start(f32[256,256]{1,0:T(8,128)S(1)} %get-tuple-element.162), channel_id=1, source_target_pairs={{0,16},{16,32},{32,48},{48,64},{64,80},{80,96},{96,112},{112,128},... | collective-permute-start | bytes 786440 | tf_op jit(solution)/shard_map/while/body/eval_jaxpr/ppermute | solution.py:15
  219.5 12.7 %collective-permute-start = (f32[256,256]{1,0:T(8,128)S(1)}, f32[256,256]{1,0:T(8,128)S(1)}, u32[]{:S(2)}, u32[]{:S(2)}) collective-permute-start(f32[256,256]{1,0:T(8,128)S(1)} %get-tuple-element.162), channel_id=1, source_target_pairs={{0,16},{16,32},{32,48},{48,64},{64,80},{80,96},{96,112},{112,128},... | collective-permute-start | bytes 786440 | tf_op jit(solution)/shard_map/while/body/eval_jaxpr/ppermute | solution.py:15
  232.3 11.8 %collective-permute-start = (f32[256,256]{1,0:T(8,128)S(1)}, f32[256,256]{1,0:T(8,128)S(1)}, u32[]{:S(2)}, u32[]{:S(2)}) collective-permute-start(f32[256,256]{1,0:T(8,128)S(1)} %get-tuple-element.162), channel_id=1, source_target_pairs={{0,16},{16,32},{32,48},{48,64},{64,80},{80,96},{96,112},{112,128},... | collective-permute-start | bytes 786440 | tf_op jit(solution)/shard_map/while/body/eval_jaxpr/ppermute | solution.py:15
  244.0 11.6 %collective-permute-start = (f32[256,256]{1,0:T(8,128)S(1)}, f32[256,256]{1,0:T(8,128)S(1)}, u32[]{:S(2)}, u32[]{:S(2)}) collective-permute-start(f32[256,256]{1,0:T(8,128)S(1)} %get-tuple-element.162), channel_id=1, source_target_pairs={{0,16},{16,32},{32,48},{48,64},{64,80},{80,96},{96,112},{112,128},... | collective-permute-start | bytes 786440 | tf_op jit(solution)/shard_map/while/body/eval_jaxpr/ppermute | solution.py:15
  255.6 11.6 %collective-permute-start = (f32[256,256]{1,0:T(8,128)S(1)}, f32[256,256]{1,0:T(8,128)S(1)}, u32[]{:S(2)}, u32[]{:S(2)}) collective-permute-start(f32[256,256]{1,0:T(8,128)S(1)} %get-tuple-element.162), channel_id=1, source_target_pairs={{0,16},{16,32},{32,48},{48,64},{64,80},{80,96},{96,112},{112,128},... | collective-permute-start | bytes 786440 | tf_op jit(solution)/shard_map/while/body/eval_jaxpr/ppermute | solution.py:15
  267.2 11.6 %collective-permute-start = (f32[256,256]{1,0:T(8,128)S(1)}, f32[256,256]{1,0:T(8,128)S(1)}, u32[]{:S(2)}, u32[]{:S(2)}) collective-permute-start(f32[256,256]{1,0:T(8,128)S(1)} %get-tuple-element.162), channel_id=1, source_target_pairs={{0,16},{16,32},{32,48},{48,64},{64,80},{80,96},{96,112},{112,128},... | collective-permute-start | bytes 786440 | tf_op jit(solution)/shard_map/while/body/eval_jaxpr/ppermute | solution.py:15
  279.6 11.6 %collective-permute-start = (f32[256,256]{1,0:T(8,128)S(1)}, f32[256,256]{1,0:T(8,128)S(1)}, u32[]{:S(2)}, u32[]{:S(2)}) collective-permute-start(f32[256,256]{1,0:T(8,128)S(1)} %get-tuple-element.162), channel_id=1, source_target_pairs={{0,16},{16,32},{32,48},{48,64},{64,80},{80,96},{96,112},{112,128},... | collective-permute-start | bytes 786440 | tf_op jit(solution)/shard_map/while/body/eval_jaxpr/ppermute | solution.py:15
  291.2 12.0 %collective-permute-start = (f32[256,256]{1,0:T(8,128)S(1)}, f32[256,256]{1,0:T(8,128)S(1)}, u32[]{:S(2)}, u32[]{:S(2)}) collective-permute-start(f32[256,256]{1,0:T(8,128)S(1)} %get-tuple-element.162), channel_id=1, source_target_pairs={{0,16},{16,32},{32,48},{48,64},{64,80},{80,96},{96,112},{112,128},... | collective-permute-start | bytes 786440 | tf_op jit(solution)/shard_map/while/body/eval_jaxpr/ppermute | solution.py:15
  303.2 13.1 %collective-permute-start = (f32[256,256]{1,0:T(8,128)S(1)}, f32[256,256]{1,0:T(8,128)S(1)}, u32[]{:S(2)}, u32[]{:S(2)}) collective-permute-start(f32[256,256]{1,0:T(8,128)S(1)} %get-tuple-element.162), channel_id=1, source_target_pairs={{0,16},{16,32},{32,48},{48,64},{64,80},{80,96},{96,112},{112,128},... | collective-permute-start | bytes 786440 | tf_op jit(solution)/shard_map/while/body/eval_jaxpr/ppermute | solution.py:15
  316.3 14.3 %collective-permute-start = (f32[256,256]{1,0:T(8,128)S(1)}, f32[256,256]{1,0:T(8,128)S(1)}, u32[]{:S(2)}, u32[]{:S(2)}) collective-permute-start(f32[256,256]{1,0:T(8,128)S(1)} %get-tuple-element.162), channel_id=1, source_target_pairs={{0,16},{16,32},{32,48},{48,64},{64,80},{80,96},{96,112},{112,128},... | collective-permute-start | bytes 786440 | tf_op jit(solution)/shard_map/while/body/eval_jaxpr/ppermute | solution.py:15
  330.5 13.5 %collective-permute-start = (f32[256,256]{1,0:T(8,128)S(1)}, f32[256,256]{1,0:T(8,128)S(1)}, u32[]{:S(2)}, u32[]{:S(2)}) collective-permute-start(f32[256,256]{1,0:T(8,128)S(1)} %get-tuple-element.162), channel_id=1, source_target_pairs={{0,16},{16,32},{32,48},{48,64},{64,80},{80,96},{96,112},{112,128},... | collective-permute-start | bytes 786440 | tf_op jit(solution)/shard_map/while/body/eval_jaxpr/ppermute | solution.py:15
  344.1 12.7 %collective-permute-start = (f32[256,256]{1,0:T(8,128)S(1)}, f32[256,256]{1,0:T(8,128)S(1)}, u32[]{:S(2)}, u32[]{:S(2)}) collective-permute-start(f32[256,256]{1,0:T(8,128)S(1)} %get-tuple-element.162), channel_id=1, source_target_pairs={{0,16},{16,32},{32,48},{48,64},{64,80},{80,96},{96,112},{112,128},... | collective-permute-start | bytes 786440 | tf_op jit(solution)/shard_map/while/body/eval_jaxpr/ppermute | solution.py:15
  356.8 11.8 %collective-permute-start = (f32[256,256]{1,0:T(8,128)S(1)}, f32[256,256]{1,0:T(8,128)S(1)}, u32[]{:S(2)}, u32[]{:S(2)}) collective-permute-start(f32[256,256]{1,0:T(8,128)S(1)} %get-tuple-element.162), channel_id=1, source_target_pairs={{0,16},{16,32},{32,48},{48,64},{64,80},{80,96},{96,112},{112,128},... | collective-permute-start | bytes 786440 | tf_op jit(solution)/shard_map/while/body/eval_jaxpr/ppermute | solution.py:15
  368.5 11.6 %collective-permute-start = (f32[256,256]{1,0:T(8,128)S(1)}, f32[256,256]{1,0:T(8,128)S(1)}, u32[]{:S(2)}, u32[]{:S(2)}) collective-permute-start(f32[256,256]{1,0:T(8,128)S(1)} %get-tuple-element.162), channel_id=1, source_target_pairs={{0,16},{16,32},{32,48},{48,64},{64,80},{80,96},{96,112},{112,128},... | collective-permute-start | bytes 786440 | tf_op jit(solution)/shard_map/while/body/eval_jaxpr/ppermute | solution.py:15
  380.1 11.6 %collective-permute-start = (f32[256,256]{1,0:T(8,128)S(1)}, f32[256,256]{1,0:T(8,128)S(1)}, u32[]{:S(2)}, u32[]{:S(2)}) collective-permute-start(f32[256,256]{1,0:T(8,128)S(1)} %get-tuple-element.162), channel_id=1, source_target_pairs={{0,16},{16,32},{32,48},{48,64},{64,80},{80,96},{96,112},{112,128},... | collective-permute-start | bytes 786440 | tf_op jit(solution)/shard_map/while/body/eval_jaxpr/ppermute | solution.py:15
  391.7 11.6 %collective-permute-start = (f32[256,256]{1,0:T(8,128)S(1)}, f32[256,256]{1,0:T(8,128)S(1)}, u32[]{:S(2)}, u32[]{:S(2)}) collective-permute-start(f32[256,256]{1,0:T(8,128)S(1)} %get-tuple-element.162), channel_id=1, source_target_pairs={{0,16},{16,32},{32,48},{48,64},{64,80},{80,96},{96,112},{112,128},... | collective-permute-start | bytes 786440 | tf_op jit(solution)/shard_map/while/body/eval_jaxpr/ppermute | solution.py:15
  403.3 11.6 %collective-permute-start = (f32[256,256]{1,0:T(8,128)S(1)}, f32[256,256]{1,0:T(8,128)S(1)}, u32[]{:S(2)}, u32[]{:S(2)}) collective-permute-start(f32[256,256]{1,0:T(8,128)S(1)} %get-tuple-element.162), channel_id=1, source_target_pairs={{0,16},{16,32},{32,48},{48,64},{64,80},{80,96},{96,112},{112,128},... | collective-permute-start | bytes 786440 | tf_op jit(solution)/shard_map/while/body/eval_jaxpr/ppermute | solution.py:15
  414.8 12.0 %collective-permute-start = (f32[256,256]{1,0:T(8,128)S(1)}, f32[256,256]{1,0:T(8,128)S(1)}, u32[]{:S(2)}, u32[]{:S(2)}) collective-permute-start(f32[256,256]{1,0:T(8,128)S(1)} %get-tuple-element.162), channel_id=1, source_target_pairs={{0,16},{16,32},{32,48},{48,64},{64,80},{80,96},{96,112},{112,128},... | collective-permute-start | bytes 786440 | tf_op jit(solution)/shard_map/while/body/eval_jaxpr/ppermute | solution.py:15
  426.9 11.6 %collective-permute-start = (f32[256,256]{1,0:T(8,128)S(1)}, f32[256,256]{1,0:T(8,128)S(1)}, u32[]{:S(2)}, u32[]{:S(2)}) collective-permute-start(f32[256,256]{1,0:T(8,128)S(1)} %get-tuple-element.162), channel_id=1, source_target_pairs={{0,16},{16,32},{32,48},{48,64},{64,80},{80,96},{96,112},{112,128},... | collective-permute-start | bytes 786440 | tf_op jit(solution)/shard_map/while/body/eval_jaxpr/ppermute | solution.py:15
  438.4 11.6 %collective-permute-start = (f32[256,256]{1,0:T(8,128)S(1)}, f32[256,256]{1,0:T(8,128)S(1)}, u32[]{:S(2)}, u32[]{:S(2)}) collective-permute-start(f32[256,256]{1,0:T(8,128)S(1)} %get-tuple-element.162), channel_id=1, source_target_pairs={{0,16},{16,32},{32,48},{48,64},{64,80},{80,96},{96,112},{112,128},... | collective-permute-start | bytes 786440 | tf_op jit(solution)/shard_map/while/body/eval_jaxpr/ppermute | solution.py:15
  450.0 11.6 %collective-permute-start = (f32[256,256]{1,0:T(8,128)S(1)}, f32[256,256]{1,0:T(8,128)S(1)}, u32[]{:S(2)}, u32[]{:S(2)}) collective-permute-start(f32[256,256]{1,0:T(8,128)S(1)} %get-tuple-element.162), channel_id=1, source_target_pairs={{0,16},{16,32},{32,48},{48,64},{64,80},{80,96},{96,112},{112,128},... | collective-permute-start | bytes 786440 | tf_op jit(solution)/shard_map/while/body/eval_jaxpr/ppermute | solution.py:15
  461.6 0.7 copy-start.1
